TPU v7x, 32 devices: a whole 2x2x4 slice. The times are simulated.
32 devices in a mesh: dp: 4 (over z), ctx: 8 (over y, x, core).
Axes of the slice: x: 2, y: 2, z: 4, core: 2. Of those that a mesh axis runs over, the one named last changes fastest.
Arguments:
- queries: bfloat16 [4, 4096, 1024], P('dp', 'ctx'), may hold values from -6 to 6
- key_vectors: bfloat16 [4, 4096, 1024], P('dp', 'ctx'), may hold values from -6 to 6
- value_vectors: bfloat16 [4, 4096, 1024], P('dp', 'ctx'), may hold values from -6 to 6
- out_grad: bfloat16 [4, 4096, 1024], P('dp', 'ctx'), may hold values from -6 to 6
- column_bias: float32 [8], replicated, may hold values from -1 to 2
- column_offsets: int32 [1], replicated, may hold values from 0 to 63
Outputs:
- attended: bfloat16 [4, 4096, 1024], P('dp', 'ctx')
- query_grad: bfloat16 [4, 4096, 1024], P('dp', 'ctx')
- key_grad: bfloat16 [4, 4096, 1024], P('dp', 'ctx')
- value_grad: bfloat16 [4, 4096, 1024], P('dp', 'ctx')
- bias_grad: float32 [8], replicated
All inputs are finite; a program needn't handle non-finite values.
Results may differ from a plain program's by a relative error of at most 0.005.
The roundings to bfloat16 on the way count: a program that leaves them out, or rounds other values in their place, can miss the bound.
Values may be sent and summed in bfloat16 or wider, within the bound.
A program may use at most 128 MiB of HBM per device.

v0:
```python
import jax
import jax.numpy as jnp
from jax import lax
from jax.sharding import PartitionSpec as P

HEADS = 8
HEAD_DIM = 128
LOCAL_BAND = 512
STRIDE = 4096
CB = 64
TOKENS_PER_SHARD = 512


def from_behind(value, axis, by):
    size = lax.axis_size(axis)
    pairs = [(i, i + by) for i in range(size) if 0 <= i + by < size]
    return lax.ppermute(value, axis, pairs)


def column_flags(positions, offsets):
    window = positions // STRIDE
    within = positions % STRIDE
    picks = window[:, None] == jnp.arange(offsets.shape[0], dtype=jnp.int32)[None, :]
    offset_at = jnp.sum(jnp.where(picks, offsets[None, :], 0), axis=1)
    return (positions >= 0) & (within // CB == offset_at)


def head_block(qh, kb, vb, kc, vc, doh, bias_h, band_ok, band_col, col_ok):
    scale = HEAD_DIM ** (-0.5)
    sb = (
        jnp.dot(qh, kb.T, preferred_element_type=jnp.float32) * scale
        + jnp.where(band_col, bias_h, 0.0)[None, :]
    )
    sc = jnp.dot(qh, kc.T, preferred_element_type=jnp.float32) * scale + bias_h
    sb = jnp.where(band_ok, sb, -jnp.inf)
    sc = jnp.where(col_ok, sc, -jnp.inf)
    top = jnp.maximum(jnp.max(sb, axis=1), jnp.max(sc, axis=1))
    pb = jnp.exp(sb - top[:, None])
    pc = jnp.exp(sc - top[:, None])
    total = jnp.sum(pb, axis=1) + jnp.sum(pc, axis=1)
    wb = pb / total[:, None]
    wc = pc / total[:, None]
    wb16 = wb.astype(jnp.bfloat16)
    wc16 = wc.astype(jnp.bfloat16)
    mixed = jnp.dot(wb16, vb, preferred_element_type=jnp.float32) + jnp.dot(
        wc16, vc, preferred_element_type=jnp.float32
    )
    oh = mixed.astype(jnp.bfloat16)
    delta = jnp.sum(doh.astype(jnp.float32) * oh.astype(jnp.float32), axis=1)
    dsb = wb * (jnp.dot(doh, vb.T, preferred_element_type=jnp.float32) - delta[:, None])
    dsc = wc * (jnp.dot(doh, vc.T, preferred_element_type=jnp.float32) - delta[:, None])
    dbias = jnp.sum(jnp.where(band_col[None, :], dsb, 0.0)) + jnp.sum(dsc)
    dsb16 = dsb.astype(jnp.bfloat16)
    dsc16 = dsc.astype(jnp.bfloat16)
    dq = (
        (
            jnp.dot(dsb16, kb, preferred_element_type=jnp.float32)
            + jnp.dot(dsc16, kc, preferred_element_type=jnp.float32)
        )
        * scale
    ).astype(jnp.bfloat16)
    dkb = jnp.dot(dsb16.T, qh, preferred_element_type=jnp.float32) * scale
    dvb = jnp.dot(wb16.T, doh, preferred_element_type=jnp.float32)
    dkc = jnp.dot(dsc16.T, qh, preferred_element_type=jnp.float32) * scale
    dvc = jnp.dot(wc16.T, doh, preferred_element_type=jnp.float32)
    return (oh, dq, dkb, dvb, dkc, dvc, dbias, top, total, delta)


def separate_heads(x):
    return x.reshape(x.shape[0], HEADS, HEAD_DIM).transpose(1, 0, 2)


def join_heads(x):
    return x.transpose(1, 0, 2).reshape(x.shape[1], HEADS * HEAD_DIM)


def per_device(queries, key_vectors, value_vectors, out_grad, column_bias, column_offsets):
    here = lax.axis_index("ctx")
    count = lax.axis_size("ctx")
    start_position = here * TOKENS_PER_SHARD
    width = queries.shape[2]
    query_rows = queries[0]
    key_rows = key_vectors[0]
    value_rows = value_vectors[0]
    grad_rows = out_grad[0]
    ncol = column_offsets.shape[0]
    block_starts = jnp.arange(ncol, dtype=jnp.int32) * STRIDE + column_offsets * CB
    colpos = jnp.repeat(block_starts, CB) + jnp.tile(jnp.arange(CB, dtype=jnp.int32), ncol)
    window = start_position // STRIDE
    own_start = window * STRIDE + column_offsets[window] * CB
    local = jnp.clip(own_start - start_position, 0, TOKENS_PER_SHARD - CB)
    piece_k = lax.dynamic_slice_in_dim(key_rows, local, CB, 0)
    piece_v = lax.dynamic_slice_in_dim(value_rows, local, CB, 0)
    pieces_k, pieces_v = (
        lax.all_gather(piece_k, "ctx", axis=0, tiled=True),
        lax.all_gather(piece_v, "ctx", axis=0, tiled=True),
    )
    owner = block_starts // TOKENS_PER_SHARD
    col_k = pieces_k.reshape(count, CB, width)[owner].reshape(ncol * CB, width)
    col_v = pieces_v.reshape(count, CB, width)[owner].reshape(ncol * CB, width)
    prev_k, prev_v = from_behind((key_rows, value_rows), "ctx", 1)
    band_k = jnp.concatenate([prev_k, key_rows], axis=0)
    band_v = jnp.concatenate([prev_v, value_rows], axis=0)
    qpos = start_position + jnp.arange(TOKENS_PER_SHARD, dtype=jnp.int32)
    kpos = start_position - LOCAL_BAND + jnp.arange(LOCAL_BAND + TOKENS_PER_SHARD, dtype=jnp.int32)
    gap = qpos[:, None] - kpos[None, :]
    band_ok = (kpos[None, :] >= 0) & (gap >= 0) & (gap < LOCAL_BAND)
    band_col = column_flags(kpos, column_offsets)
    col_ok = colpos[None, :] <= qpos[:, None] - LOCAL_BAND

    def per_head(items):
        return head_block(
            items[0],
            items[1],
            items[2],
            items[3],
            items[4],
            items[5],
            items[6],
            band_ok,
            band_col,
            col_ok,
        )

    results = lax.map(
        per_head,
        (
            separate_heads(query_rows),
            separate_heads(band_k),
            separate_heads(band_v),
            separate_heads(col_k),
            separate_heads(col_v),
            separate_heads(grad_rows),
            column_bias,
        ),
    )
    oh, dq, dkb, dvb, dkc, dvc, dbias, top, total, delta = results
    attended = join_heads(oh)
    query_grad = join_heads(dq)
    dk_band = join_heads(dkb)
    dv_band = join_heads(dvb)
    own_dk = dk_band[dk_band.shape[0] - TOKENS_PER_SHARD :]
    own_dv = dv_band[dv_band.shape[0] - TOKENS_PER_SHARD :]
    back_k, back_v = from_behind((dk_band[:LOCAL_BAND], dv_band[:LOCAL_BAND]), "ctx", -1)
    own_dk = own_dk.at[TOKENS_PER_SHARD - LOCAL_BAND :].add(back_k)
    own_dv = own_dv.at[TOKENS_PER_SHARD - LOCAL_BAND :].add(back_v)
    summed_k, summed_v = lax.psum((join_heads(dkc), join_heads(dvc)), "ctx")
    flags = column_flags(qpos, column_offsets)
    source = jnp.clip(qpos // STRIDE * CB + qpos % CB, 0, ncol * CB - 1)
    own_dk = own_dk + jnp.where(flags[:, None], summed_k[source], 0.0)
    own_dv = own_dv + jnp.where(flags[:, None], summed_v[source], 0.0)
    bias_grad = lax.psum(dbias, ("dp", "ctx"))
    return (
        attended[None],
        query_grad[None],
        own_dk.astype(jnp.bfloat16)[None],
        own_dv.astype(jnp.bfloat16)[None],
        bias_grad,
    )


def solution(mesh):
    placed = (
        P("dp", "ctx", None),
        P("dp", "ctx", None),
        P("dp", "ctx", None),
        P("dp", "ctx", None),
        P(),
        P(),
    )
    return jax.shard_map(
        per_device,
        mesh=mesh,
        in_specs=placed,
        out_specs=(
            P("dp", "ctx", None),
            P("dp", "ctx", None),
            P("dp", "ctx", None),
            P("dp", "ctx", None),
            P(),
        ),
        check_vma=False,
    )
```

profile of v0, /device:TPU:0, one launch (start us, length us, event | category | flops | bytes accessed | tf_op | source)
XLA Modules:
  0.0 354.4 jit_solution(14615889557479074196)
XLA Ops:
  12.8 3.3 collective-permute-start
  16.7 4.5 %collective-permute-start.1 = (bf16[512,1024]{0,1:T(8,128)(2,1)S(1)}, bf16[512,1024]{0,1:T(8,128)(2,1)}, u32[]{:S(2)}, u32[]{:S(2)}) collective-permute-start(bf16[512,1024]{0,1:T(8,128)(2,1)S(1)} %bitcast.242), channel_id=1, source_target_pairs={{0,1},{1,2},{2,3},{3,4},{4,5},{5,6},{6,7},{8,9},{9,10},{10,11},{11... | collective-permute-start | bytes 3145736 | tf_op jit(solution)/shard_map/ppermute | solution.py:17
  22.7 2.3 copy.26
  25.1 2.9 maximum_bitcast_fusion
  28.0 2.9 maximum_bitcast_fusion.1
  30.9 7.3 %all-gather.7.cloned.1.call-done = bf16[1,512,1024]{2,1,0:T(8,128)(2,1)} async-done(((bf16[1,64,1024]{2,1,0:T(8,128)(2,1)}), bf16[1,512,1024]{2,1,0:T(8,128)(2,1)}) %all-gather.7.cloned.1.call-update) | async-done | bytes 1048592 | tf_op jit(solution)/shard_map/all_gather | solution.py:96
  38.2 25.5 %all-gather.5.cloned.1.call-done = bf16[1,512,1024]{2,1,0:T(8,128)(2,1)} async-done(((bf16[1,64,1024]{2,1,0:T(8,128)(2,1)}), bf16[1,512,1024]{2,1,0:T(8,128)(2,1)}) %all-gather.5.cloned.1.call-update) | async-done | bytes 1048592 | tf_op jit(solution)/shard_map/all_gather | solution.py:95
  65.4 169.8 %while.29 = (s32[]{:T(128)}, bf16[8,512,128]{1,2,0:T(8,128)(2,1)}, bf16[8,512,128]{2,1,0:T(8,128)(2,1)}, f32[8,1024,128]{2,1,0:T(8,128)}, f32[8,1024,128]{2,1,0:...) while((s32[]{:T(128)}, bf16[8,512,128]{1,2,0:T(8,128)(2,1)}, ...), condition=%wide.region_8.9_spmd.clone, body=%wide.region_0.8_spmd.clone.sunk | while | flops 869654016 | bytes 19551504 | solution.py:125
  77.8 2.5 select_reduce_fusion.2
  99.0 2.5 select_reduce_fusion.2
  109.8 2.0 fusion.160
  120.2 2.5 select_reduce_fusion.2
  141.4 2.5 select_reduce_fusion.2
  162.7 2.5 select_reduce_fusion.2
  183.9 2.5 select_reduce_fusion.2
  205.1 2.5 select_reduce_fusion.2
  215.9 2.0 fusion.160
  226.4 2.5 select_reduce_fusion.2
  235.3 4.0 %slice_bitcast_fusion.3 = (f32[8,64,8,128]{3,2,1,0:T(8,128)}, f32[8,64,8,128]{3,2,1,0:T(8,128)S(1)}) fusion(f32[1024,8,128]{2,0,1:T(8,128)} %bitcast.240), kind=kLoop, calls=%fused_computation.130 | loop fusion | bytes 8388608
  248.4 79.4 %psum.23 = f32[8]{0:T(128)} all-reduce(f32[8]{0:T(128)S(1)} %get-tuple-element.149), channel_id=1, replica_groups=mesh['dp'=4,'ctx'=8] {'dp','ctx'}, use_global_device_ids=true, to_apply=%region_11.12 | all-reduce | flops 8 | bytes 64 | tf_op jit(solution)/shard_map/psum | solution.py:152
  331.1 4.3 %all-reduce.3.cloned.1.call-done = (f32[64,1024]{1,0:T(8,128)}, f32[64,1024]{1,0:T(8,128)}) async-done(((f32[64,1024]{1,0:T(8,128)}, f32[64,1024]{1,0:T(8,128)}), (f32[64,1024]{1,0:T(8,128)}, f32[64,1024]{1,0:T(8,128)})) %all-reduce.3.cloned.1.call-update) | async-done | bytes 524304 | tf_op jit(solution)/shard_map/psum | solution.py:147
  335.3 3.8 %gather_fusion = f32[512,1024]{1,0:T(8,128)S(1)} fusion(f32[64,1024]{1,0:T(8,128)} %get-tuple-element.315, s32[1024]{0:T(1024)S(1)} %pad_clamp_fusion), kind=kCustom, calls=%fused_computation | custom fusion | bytes 4196352 | tf_op jit(solution)/shard_map/gather | solution.py:150
  339.2 2.7 gather_fusion.1
  341.8 6.0 %fusion.99 = (bf16[1,512,1024]{2,1,0:T(8,128)(2,1)}, bf16[1,512,1024]{2,1,0:T(8,128)(2,1)}) fusion(f32[512,1024]{1,0:T(8,128)} %gather_fusion.1, f32[512,1024]{1,0:T(8,128)} %collective-permute-done.3, f32[8,64,8,128]{3,2,1,0:T(8,128)} %get-tuple-element.327, pred[512]{0:T(512)(128)(4,1)S(1)} %fusion.108, f32[512,1024]{1,0:T(8,128)S(1)} %gather_fusion, ...), kind=kLoop, calls=%fused_computation.134 | loop fusion | flops 4194304 | bytes 14680576 | tf_op jit(solution)/shard_map/convert_element_type | solution.py:157
  (220 shorter events, 157.1 us)
Async XLA Ops:
  7.2 9.0 %copy-start.3 = (bf16[1,512,1024]{2,1,0:T(8,128)(2,1)S(1)}, bf16[1,512,1024]{2,1,0:T(8,128)(2,1)}, u32[]{:S(2)}) copy-start(bf16[1,512,1024]{2,1,0:T(8,128)(2,1)} %param.18) | copy-start | bytes 3145732
  7.2 31.1 %all-gather.7.cloned.1.call-start = ((), (), s32[]{:S(2)}) async-start(), calls=%async_computation.1 | async-start | bytes 1179648 | tf_op jit(solution)/shard_map/all_gather | solution.py:96
  9.6 54.1 %all-gather.5.cloned.1.call-start = ((), (), s32[]{:S(2)}) async-start(), calls=%async_computation | async-start | bytes 1179648 | tf_op jit(solution)/shard_map/all_gather | solution.py:95
  11.2 324.1 %all-reduce.3.cloned.1.call-start = ((), (), s32[]{:S(2)}) async-start(), calls=%async_computation.2 | async-start | bytes 1048576 | tf_op jit(solution)/shard_map/psum | solution.py:147
  12.8 12.3 %collective-permute-start = (bf16[512,1024]{0,1:T(8,128)(2,1)S(1)}, bf16[512,1024]{0,1:T(8,128)(2,1)}, u32[]{:S(2)}, u32[]{:S(2)}) collective-permute-start(bf16[512,1024]{0,1:T(8,128)(2,1)S(1)} %bitcast.244), channel_id=1, source_target_pairs={{0,1},{1,2},{2,3},{3,4},{4,5},{5,6},{6,7},{8,9},{9,10},{10,11},{11... | collective-permute-start | bytes 3145736 | tf_op jit(solution)/shard_map/ppermute | solution.py:17
  16.7 11.3 %collective-permute-start.1 = (bf16[512,1024]{0,1:T(8,128)(2,1)S(1)}, bf16[512,1024]{0,1:T(8,128)(2,1)}, u32[]{:S(2)}, u32[]{:S(2)}) collective-permute-start(bf16[512,1024]{0,1:T(8,128)(2,1)S(1)} %bitcast.242), channel_id=1, source_target_pairs={{0,1},{1,2},{2,3},{3,4},{4,5},{5,6},{6,7},{8,9},{9,10},{10,11},{11... | collective-permute-start | bytes 3145736 | tf_op jit(solution)/shard_map/ppermute | solution.py:17
  28.0 37.5 %copy-start.2 = (bf16[1,512,1024]{1,2,0:T(8,128)(2,1)S(1)}, bf16[1,512,1024]{1,2,0:T(8,128)(2,1)}, u32[]{:S(2)}) copy-start(bf16[1,512,1024]{1,2,0:T(8,128)(2,1)} %copy.26) | copy-start | bytes 3145732
  28.0 37.5 %copy-start.8 = (f32[8]{0:T(128)S(1)}, f32[8]{0:T(128)}, u32[]{:S(2)}) copy-start(f32[8]{0:T(128)} %param.20) | copy-start | bytes 100
  239.2 3.0 copy-start.1
  240.8 101.0 %collective-permute-start.2 = (f32[512,1024]{1,0:T(8,128)}, f32[512,1024]{1,0:T(8,128)}, u32[]{:S(2)}, u32[]{:S(2)}) collective-permute-start(f32[512,1024]{1,0:T(8,128)} %bitcast.178), channel_id=1, source_target_pairs={{1,0},{2,1},{3,2},{4,3},{5,4},{6,5},{7,6},{9,8},{10,9},{11,10},{12... | collective-permute-start | bytes 6291464 | tf_op jit(solution)/shard_map/ppermute | solution.py:17
  243.9 2.9 copy-start.7
  243.9 3.7 %copy-start.6 = (f32[8,64,128]{2,1,0:T(8,128)S(1)}, f32[8,64,128]{2,1,0:T(8,128)}, u32[]{:S(2)}) copy-start(f32[8,64,128]{2,1,0:T(8,128)} %get-tuple-element.146) | copy-start | bytes 786436
  243.9 83.9 %copy-start.5 = (bf16[8,512,128]{2,1,0:T(8,128)(2,1)S(1)}, bf16[8,512,128]{2,1,0:T(8,128)(2,1)}, u32[]{:S(2)}) copy-start(bf16[8,512,128]{2,1,0:T(8,128)(2,1)} %get-tuple-element.144) | copy-start | bytes 3145732
  245.5 96.3 %collective-permute-start.3 = (f32[512,1024]{1,0:T(8,128)}, f32[512,1024]{1,0:T(8,128)}, u32[]{:S(2)}, u32[]{:S(2)}) collective-permute-start(f32[512,1024]{1,0:T(8,128)} %bitcast.177), channel_id=1, source_target_pairs={{1,0},{2,1},{3,2},{4,3},{5,4},{6,5},{7,6},{9,8},{10,9},{11,10},{12... | collective-permute-start | bytes 6291464 | tf_op jit(solution)/shard_map/ppermute | solution.py:17
  327.8 2.0 copy-start.4
  335.3 3.8 %copy-start = (f32[64,1024]{1,0:T(8,128)S(1)}, f32[64,1024]{1,0:T(8,128)}, u32[]{:S(2)}) copy-start(f32[64,1024]{1,0:T(8,128)} %get-tuple-element.316) | copy-start | bytes 786436
Sparse Core Ops, SparseCore 0:
  9.9 28.2 all-gather.6
  40.1 23.5 all-gather.4
  248.4 86.8 all-reduce.2
where the time goes:
time: 357 us; the launch traced here: 354 us
  matrix products  133 us (37%)
  blocking collectives  79.4 us (22%)
  waiting for transfers between devices  37.1 us (10%)
  local copies, waits for them, and re-layouts  36.4 us (10%)
  other arithmetic  32.7 us (9%)
  between operations  14.7 us (4%)
  starting transfers between devices  10.7 us (3%)
  loops' own time  10 us (3%)
    psum x1, blocking collectives, per_device(): bias_grad = lax.psum(dbias, ('dp', 'ctx'))  79.4 us
    all_gather x1, waiting for transfers between devices, per_device(): lax.all_gather(piece_k, 'ctx', axis=0, tiled=True)  25.5 us
    dot_general x8, matrix products, head_block(): jnp.dot(doh, vb.T, preferred_element_type=jnp.float32) - delta[:, None]  19.7 us
    dot_general x8, matrix products, head_block(): jnp.dot(qh, kb.T, preferred_element_type=jnp.float32) * scale  15.9 us
    unnamed x29, local copies, waits for them, and re-layouts  13.2 us
    dot_general x8, matrix products, head_block(): jnp.dot(wb16, vb, preferred_element_type=jnp.float32)  12.9 us
    dot_general x8, matrix products, head_block(): jnp.dot(wc16, vc, preferred_element_type=jnp.float32)  12.9 us
    dot_general x8, matrix products, head_block(): dvb = jnp.dot(wb16.T, doh, preferred_element_type=jnp.float32)  12.7 us
  transfers between devices with their start and end apart: 7, of which 3 were waited for; matrix products, arithmetic and copies ran while one was open for 8% of the time, Pallas kernels for 0%

commit v1 on v0

--- a/solution.py
+++ b/solution.py
@@ -9,6 +9,23 @@
 STRIDE = 4096
 CB = 64
 TOKENS_PER_SHARD = 512
+
+
+def show_views(slab_in):
+    right_arr, main, out_arr = (lax.axis_size("ctx"), lax.axis_index("ctx"), slab_in.shape[0])
+    tmp, k_now = (slab_in, 1)
+    while k_now < right_arr:
+        tmp = jnp.concatenate(
+            [
+                tmp,
+                lax.ppermute(
+                    tmp, "ctx", [(idx, (idx - k_now) % right_arr) for idx in range(right_arr)]
+                ),
+            ],
+            0,
+        )
+        k_now = 2 * k_now
+    return jnp.roll(tmp, main * out_arr, 0)
 
 
 def from_behind(value, axis, by):
@@ -91,10 +108,7 @@
     local = jnp.clip(own_start - start_position, 0, TOKENS_PER_SHARD - CB)
     piece_k = lax.dynamic_slice_in_dim(key_rows, local, CB, 0)
     piece_v = lax.dynamic_slice_in_dim(value_rows, local, CB, 0)
-    pieces_k, pieces_v = (
-        lax.all_gather(piece_k, "ctx", axis=0, tiled=True),
-        lax.all_gather(piece_v, "ctx", axis=0, tiled=True),
-    )
+    pieces_k, pieces_v = (show_views(piece_k), lax.all_gather(piece_v, "ctx", axis=0, tiled=True))
     owner = block_starts // TOKENS_PER_SHARD
     col_k = pieces_k.reshape(count, CB, width)[owner].reshape(ncol * CB, width)
     col_v = pieces_v.reshape(count, CB, width)[owner].reshape(ncol * CB, width)

time: 357 us -> 368 us (1.031)
  local copies, waits for them, and re-layouts: 36.4 us -> 45.3 us
  waiting for transfers between devices: 37.1 us -> 31.9 us
    ppermute x0 -> x3, waiting for transfers between devices: none -> 28.8 us  [show_views(): lax.ppermute(tmp, 'ctx', [(idx, (idx - k_now) % right_arr) for idx in ran...]
    all_gather x1 -> x0, waiting for transfers between devices: 25.5 us -> none  [per_device(): lax.all_gather(piece_k, 'ctx', axis=0, tiled=True)]
    unnamed x29 -> x44, local copies, waits for them, and re-layouts: 13.2 us -> 20.6 us
    all_gather x1, waiting for transfers between devices: 7.35 us -> 0.01 us  [per_device(): lax.all_gather(piece_v, 'ctx', axis=0, tiled=True)]
    ppermute x0 -> x3, starting transfers between devices: none -> 3.97 us  [show_views(): lax.ppermute(tmp, 'ctx', [(idx, (idx - k_now) % right_arr) for idx in ran...]
  transfers between devices with their start and end apart: 7 -> 9, of which waited for: 3 -> 3; matrix products, arithmetic and copies ran while one was open for 8% -> 10% of each run, Pallas kernels for 0% -> 0%
where the time goes in v1:
time: 368 us; the launch traced here: 365 us
  matrix products  133 us (36%)
  blocking collectives  80.6 us (22%)
  local copies, waits for them, and re-layouts  45.3 us (12%)
  other arithmetic  34.9 us (9%)
  waiting for transfers between devices  31.9 us (9%)
  between operations  15 us (4%)
  starting transfers between devices  14.3 us (4%)
  loops' own time  10 us (3%)
    psum x1, blocking collectives, per_device(): bias_grad = lax.psum(dbias, ('dp', 'ctx'))  80.6 us
    ppermute x3, waiting for transfers between devices, show_views(): lax.ppermute(tmp, 'ctx', [(idx, (idx - k_now) % right_arr) for idx in ran...  28.8 us
    unnamed x44, local copies, waits for them, and re-layouts  20.6 us
    dot_general x8, matrix products, head_block(): jnp.dot(doh, vb.T, preferred_element_type=jnp.float32) - delta[:, None]  19.7 us
    dot_general x8, matrix products, head_block(): jnp.dot(qh, kb.T, preferred_element_type=jnp.float32) * scale  15.9 us
    dot_general x8, matrix products, head_block(): jnp.dot(wb16, vb, preferred_element_type=jnp.float32)  12.9 us
    dot_general x8, matrix products, head_block(): jnp.dot(wc16, vc, preferred_element_type=jnp.float32)  12.9 us
    dot_general x8, matrix products, head_block(): dvb = jnp.dot(wb16.T, doh, preferred_element_type=jnp.float32)  12.7 us
  transfers between devices with their start and end apart: 9, of which 3 were waited for; matrix products, arithmetic and copies ran while one was open for 10% of the time, Pallas kernels for 0%

profile of v1, /device:TPU:0, one launch (start us, length us, event | category | flops | bytes accessed | tf_op | source)
XLA Modules:
  0.0 365.2 jit_solution(11314886545845575888)
XLA Ops:
  9.6 3.3 collective-permute-start.1
  12.9 2.5 collective-permute-done.1
  20.5 5.2 %collective-permute-start = (bf16[512,1024]{0,1:T(8,128)(2,1)S(1)}, bf16[512,1024]{0,1:T(8,128)(2,1)}, u32[]{:S(2)}, u32[]{:S(2)}) collective-permute-start(bf16[512,1024]{0,1:T(8,128)(2,1)S(1)} %bitcast.247), channel_id=1, source_target_pairs={{0,1},{1,2},{2,3},{3,4},{4,5},{5,6},{6,7},{8,9},{9,10},{10,11},{11... | collective-permute-start | bytes 3145736 | tf_op jit(solution)/shard_map/ppermute | solution.py:34
  26.3 2.3 collective-permute-start.4
  30.1 2.3 copy.26
  36.3 26.3 %collective-permute-done.3 = bf16[256,1024]{1,0:T(8,128)(2,1)S(1)} collective-permute-done((bf16[256,1024]{1,0:T(8,128)(2,1)S(1)}, bf16[256,1024]{1,0:T(8,128)(2,1)S(1)}, u32[]{:S(2)}, u32[]{:S(2)}) %collective-permute-start.3) | collective-permute-done | bytes 524320 | tf_op jit(solution)/shard_map/ppermute | solution.py:21
  66.4 2.3 constant_dynamic-slice_fusion.1
  68.6 2.9 maximum_bitcast_fusion
  71.5 2.9 maximum_bitcast_fusion.1
  76.2 169.6 %while.29 = (s32[]{:T(128)}, bf16[8,512,128]{1,2,0:T(8,128)(2,1)}, bf16[8,512,128]{2,1,0:T(8,128)(2,1)}, f32[8,1024,128]{2,1,0:T(8,128)}, f32[8,1024,128]{2,1,0:...) while((s32[]{:T(128)}, bf16[8,512,128]{1,2,0:T(8,128)(2,1)}, ...), condition=%wide.region_8.9_spmd.clone, body=%wide.region_0.8_spmd.clone.sunk | while | flops 869654016 | bytes 19551504 | solution.py:139
  88.5 2.5 select_reduce_fusion.2
  109.7 2.5 select_reduce_fusion.2
  131.0 2.5 select_reduce_fusion.2
  152.2 2.5 select_reduce_fusion.2
  173.4 2.5 select_reduce_fusion.2
  194.6 2.5 select_reduce_fusion.2
  215.8 2.5 select_reduce_fusion.2
  237.0 2.5 select_reduce_fusion.2
  245.9 4.0 %slice_bitcast_fusion.3 = (f32[8,64,8,128]{3,2,1,0:T(8,128)}, f32[8,64,8,128]{3,2,1,0:T(8,128)S(1)}) fusion(f32[1024,8,128]{2,0,1:T(8,128)} %bitcast.243), kind=kLoop, calls=%fused_computation.130 | loop fusion | bytes 8388608
  259.0 80.6 %psum.23 = f32[8]{0:T(128)} all-reduce(f32[8]{0:T(128)S(1)} %get-tuple-element.149), channel_id=1, replica_groups=mesh['dp'=4,'ctx'=8] {'dp','ctx'}, use_global_device_ids=true, to_apply=%region_11.12 | all-reduce | flops 8 | bytes 64 | tf_op jit(solution)/shard_map/psum | solution.py:166
  342.8 3.0 all-reduce.3.cloned.1.call-done
  345.8 3.8 %gather_fusion = f32[512,1024]{1,0:T(8,128)S(1)} fusion(f32[64,1024]{1,0:T(8,128)} %get-tuple-element.315, s32[1024]{0:T(1024)S(1)} %pad_clamp_fusion), kind=kCustom, calls=%fused_computation | custom fusion | bytes 4196352 | tf_op jit(solution)/shard_map/gather | solution.py:164
  349.7 2.7 gather_fusion.1
  352.3 6.0 %fusion.99 = (bf16[1,512,1024]{2,1,0:T(8,128)(2,1)}, bf16[1,512,1024]{2,1,0:T(8,128)(2,1)}) fusion(f32[512,1024]{1,0:T(8,128)} %gather_fusion.1, f32[512,1024]{1,0:T(8,128)} %collective-permute-done.6, f32[8,64,8,128]{3,2,1,0:T(8,128)} %get-tuple-element.329, pred[512]{0:T(512)(128)(4,1)S(1)} %fusion.108, f32[512,1024]{1,0:T(8,128)S(1)} %gather_fusion, ...), kind=kLoop, calls=%fused_computation.134 | loop fusion | flops 4194304 | bytes 14680576 | tf_op jit(solution)/shard_map/convert_element_type | solution.py:171
  (241 shorter events, 170.5 us)
Async XLA Ops:
  7.2 18.6 %copy-start.5 = (bf16[1,512,1024]{2,1,0:T(8,128)(2,1)S(1)}, bf16[1,512,1024]{2,1,0:T(8,128)(2,1)}, u32[]{:S(2)}) copy-start(bf16[1,512,1024]{2,1,0:T(8,128)(2,1)} %param.18) | copy-start | bytes 3145732
  7.2 67.3 %all-gather.3.cloned.1.call-start = ((), (), s32[]{:S(2)}) async-start(), calls=%async_computation | async-start | bytes 1179648 | tf_op jit(solution)/shard_map/all_gather | solution.py:111
  9.6 5.9 %collective-permute-start.1 = (bf16[64,1024]{1,0:T(8,128)(2,1)S(1)}, bf16[64,1024]{1,0:T(8,128)(2,1)S(1)}, u32[]{:S(2)}, u32[]{:S(2)}) collective-permute-start(bf16[64,1024]{1,0:T(8,128)(2,1)S(1)} %get-tuple-element.318), channel_id=1, source_target_pairs={{0,7},{1,0},{2,1},{3,2},{4,3},{5,4},{6,5},{7,6},{8,15},{9,8},{10,9... | collective-permute-start | bytes 393224 | tf_op jit(solution)/shard_map/ppermute | solution.py:21
  15.4 0.6 copy-start.3
  16.8 15.6 %collective-permute-start.2 = (bf16[128,1024]{1,0:T(8,128)(2,1)}, bf16[128,1024]{1,0:T(8,128)(2,1)S(1)}, u32[]{:S(2)}, u32[]{:S(2)}) collective-permute-start(bf16[128,1024]{1,0:T(8,128)(2,1)} %pad_maximum_fusion.1), channel_id=1, source_target_pairs={{0,6},{1,7},{2,0},{3,1},{4,2},{5,3},{6,4},{7,5},{8,14},{9,15},{10,... | collective-permute-start | bytes 786440 | tf_op jit(solution)/shard_map/ppermute | solution.py:21
  19.0 326.9 %all-reduce.3.cloned.1.call-start = ((), (), s32[]{:S(2)}) async-start(), calls=%async_computation.1 | async-start | bytes 1048576 | tf_op jit(solution)/shard_map/psum | solution.py:161
  20.5 48.1 %collective-permute-start = (bf16[512,1024]{0,1:T(8,128)(2,1)S(1)}, bf16[512,1024]{0,1:T(8,128)(2,1)}, u32[]{:S(2)}, u32[]{:S(2)}) collective-permute-start(bf16[512,1024]{0,1:T(8,128)(2,1)S(1)} %bitcast.247), channel_id=1, source_target_pairs={{0,1},{1,2},{2,3},{3,4},{4,5},{5,6},{6,7},{8,9},{9,10},{10,11},{11... | collective-permute-start | bytes 3145736 | tf_op jit(solution)/shard_map/ppermute | solution.py:34
  26.3 45.2 %collective-permute-start.4 = (bf16[512,1024]{0,1:T(8,128)(2,1)S(1)}, bf16[512,1024]{0,1:T(8,128)(2,1)}, u32[]{:S(2)}, u32[]{:S(2)}) collective-permute-start(bf16[512,1024]{0,1:T(8,128)(2,1)S(1)} %bitcast.245), channel_id=1, source_target_pairs={{0,1},{1,2},{2,3},{3,4},{4,5},{5,6},{6,7},{8,9},{9,10},{10,11},{11... | collective-permute-start | bytes 3145736 | tf_op jit(solution)/shard_map/ppermute | solution.py:34
  32.4 31.8 %copy-start.4 = (bf16[64,1024]{1,0:T(8,128)(2,1)S(1)}, bf16[64,1024]{1,0:T(8,128)(2,1)}, u32[]{:S(2)}) copy-start(bf16[64,1024]{1,0:T(8,128)(2,1)} %copy-done.3) | copy-start | bytes 393220
  33.4 29.2 %collective-permute-start.3 = (bf16[256,1024]{1,0:T(8,128)(2,1)S(1)}, bf16[256,1024]{1,0:T(8,128)(2,1)S(1)}, u32[]{:S(2)}, u32[]{:S(2)}) collective-permute-start(bf16[256,1024]{1,0:T(8,128)(2,1)S(1)} %pad_maximum_fusion), channel_id=1, source_target_pairs={{0,4},{1,5},{2,6},{3,7},{4,0},{5,1},{6,2},{7,3},{8,12},{9,13},{10,... | collective-permute-start | bytes 1572872 | tf_op jit(solution)/shard_map/ppermute | solution.py:21
  71.5 4.7 %copy-start.2 = (bf16[1,512,1024]{1,2,0:T(8,128)(2,1)S(1)}, bf16[1,512,1024]{1,2,0:T(8,128)(2,1)}, u32[]{:S(2)}) copy-start(bf16[1,512,1024]{1,2,0:T(8,128)(2,1)} %copy.26) | copy-start | bytes 3145732
  71.5 4.7 %copy-start.10 = (f32[8]{0:T(128)S(1)}, f32[8]{0:T(128)}, u32[]{:S(2)}) copy-start(f32[8]{0:T(128)} %param.20) | copy-start | bytes 100
  71.5 4.7 %copy-start.11 = (pred[1024]{0:T(1024)(128)(4,1)S(1)}, pred[1024]{0:T(1024)(128)(4,1)}, u32[]{:S(2)}) copy-start(pred[1024]{0:T(1024)(128)(4,1)} %broadcast_compare_fusion) | copy-start | bytes 3076
  71.5 4.7 %copy-start.12 = (f32[8]{0:T(128)S(1)}, f32[8]{0:T(128)}, u32[]{:S(2)}) copy-start(f32[8]{0:T(128)} %custom-call.11) | copy-start | bytes 100
  249.8 3.0 copy-start.1
  251.4 100.9 %collective-permute-start.5 = (f32[512,1024]{1,0:T(8,128)}, f32[512,1024]{1,0:T(8,128)}, u32[]{:S(2)}, u32[]{:S(2)}) collective-permute-start(f32[512,1024]{1,0:T(8,128)} %bitcast.181), channel_id=1, source_target_pairs={{1,0},{2,1},{3,2},{4,3},{5,4},{6,5},{7,6},{9,8},{10,9},{11,10},{12... | collective-permute-start | bytes 6291464 | tf_op jit(solution)/shard_map/ppermute | solution.py:34
  254.5 2.9 copy-start.8
  254.5 3.7 %copy-start.9 = (f32[8,64,128]{2,1,0:T(8,128)S(1)}, f32[8,64,128]{2,1,0:T(8,128)}, u32[]{:S(2)}) copy-start(f32[8,64,128]{2,1,0:T(8,128)} %get-tuple-element.146) | copy-start | bytes 786436
  254.5 85.0 %copy-start.7 = (bf16[8,512,128]{2,1,0:T(8,128)(2,1)S(1)}, bf16[8,512,128]{2,1,0:T(8,128)(2,1)}, u32[]{:S(2)}) copy-start(bf16[8,512,128]{2,1,0:T(8,128)(2,1)} %get-tuple-element.144) | copy-start | bytes 3145732
  256.1 96.2 %collective-permute-start.6 = (f32[512,1024]{1,0:T(8,128)}, f32[512,1024]{1,0:T(8,128)}, u32[]{:S(2)}, u32[]{:S(2)}) collective-permute-start(f32[512,1024]{1,0:T(8,128)} %bitcast.180), channel_id=1, source_target_pairs={{1,0},{2,1},{3,2},{4,3},{5,4},{6,5},{7,6},{9,8},{10,9},{11,10},{12... | collective-permute-start | bytes 6291464 | tf_op jit(solution)/shard_map/ppermute | solution.py:34
  339.5 2.0 copy-start.6
  345.8 3.8 %copy-start = (f32[64,1024]{1,0:T(8,128)S(1)}, f32[64,1024]{1,0:T(8,128)}, u32[]{:S(2)}) copy-start(f32[64,1024]{1,0:T(8,128)} %get-tuple-element.316) | copy-start | bytes 786436
Sparse Core Ops, SparseCore 0:
  19.1 35.1 all-gather.2
  259.0 86.7 all-reduce.2
